TPU v7x, 32 devices: a whole 2x2x4 slice. The times are simulated.
32 devices in a mesh: axial: 4 (over z), azim: 8 (over y, x, core).
Axes of the slice: x: 2, y: 2, z: 4, core: 2. Of those that a mesh axis runs over, the one named last changes fastest.
Arguments:
- fields: float32 [4096, 4, 1024], P(('axial', 'azim')), may hold values from -6 to 6
- new_owner: int32 [4096, 1], P(('axial', 'azim')), may hold values from 0 to 31; in each aligned block of 128 rows (0 to 127, 128 to 255, ...) at most 6 rows name the same one
- leaflet: bfloat16 [64, 128, 2048], P(None, 'axial', 'azim'), may hold values from -6 to 6
- stiffness: bfloat16 [64, 64], replicated, may hold values from -0.75 to 0.75
- coarse: float32 [2048, 256], P(('axial', 'azim')), may hold values from -6 to 6
- coarse_of_slot: int32 [6144], P(('axial', 'azim')), may hold values from 0 to 63
- viscosity: float32 [4], replicated, may hold values from 0.02 to 0.2
Outputs:
- regridded: float32 [6144, 4, 1024], P(('axial', 'azim'))
Inputs may be any that keep to these rules, and one draw needn't show every extreme that they name: `new_owner`: among the patches of one device, at most 6 share a new owner; in some device's patches exactly 6 do.
All inputs are finite; a program needn't handle non-finite values.
Results may differ from a plain program's by a relative error of at most 0.004.
Values may be sent and summed in bfloat16 or wider, within the bound.
A program may use at most 64 MiB of HBM per device.

v0:
```python
import jax
import jax.numpy as jnp
from jax import lax
from jax.sharding import PartitionSpec as P

PC = 64
FIELDS = 4
STEPS = 2


SPREAD = 0.25


def padded(shard, sides, width, wrap):
    for axis, dim in sides:
        size, length = (lax.axis_size(axis), shard.shape[dim])
        up = [(i, (i + 1) % size) for i in range(size if wrap else size - 1)]
        down = [(j, i) for i, j in up]
        last = lax.slice_in_dim(shard, length - width, length, axis=dim)
        initial = lax.slice_in_dim(shard, 0, width, axis=dim)
        before = lax.ppermute(last, axis, up)
        after = lax.ppermute(initial, axis, down)
        shard = jnp.concatenate([before, shard, after], axis=dim)
    return shard


def interp_table(coarse_cols):
    fine_col = jnp.arange(2 * coarse_cols)
    nearest = fine_col // 2
    second = jnp.where(
        fine_col % 2 == 0, jnp.maximum(nearest - 1, 0), jnp.minimum(nearest + 1, coarse_cols - 1)
    )
    coarse_row = jnp.arange(coarse_cols)[:, None]
    return 0.75 * (coarse_row == nearest[None, :]).astype(jnp.float32) + 0.25 * (
        coarse_row == second[None, :]
    ).astype(jnp.float32)


def viscous(state, ghosts, viscosity):
    row_pad = jnp.concatenate([ghosts[:, :, 0:1, :], state, ghosts[:, :, 1:2, :]], axis=2)
    col_pad = jnp.pad(state, ((0, 0), (0, 0), (0, 0), (1, 1)))
    laplace = (
        row_pad[:, :, 2:, :]
        + row_pad[:, :, :-2, :]
        + col_pad[:, :, :, 2:]
        + col_pad[:, :, :, :-2]
        - 4.0 * state
    )
    return state + viscosity[None, :, None, None] * laplace


def leaflet_sheets(leaflet, stiffness):
    records, rows_axial, cols_azim = leaflet.shape
    patch_cols = cols_azim // PC
    points = leaflet.astype(jnp.float32)
    axial_pad = padded(leaflet, (("axial", 1),), 1, False).astype(jnp.float32)
    azim_pad = padded(leaflet, (("azim", 2),), 1, True).astype(jnp.float32)
    laplace = (
        axial_pad[:, 2:, :]
        + axial_pad[:, :-2, :]
        + azim_pad[:, :, :-2]
        + azim_pad[:, :, 2:]
        - 4.0 * points
    )
    laplace = laplace.astype(jnp.bfloat16)
    tension = jnp.dot(
        stiffness, laplace.reshape(records, -1), preferred_element_type=jnp.float32
    ).astype(jnp.bfloat16)
    tension = tension.reshape(records, rows_axial, patch_cols, PC).transpose(1, 2, 0, 3)
    return tension.reshape(rows_axial * patch_cols, FIELDS, records // FIELDS * PC)


def place_slots(values, target, total_slots):
    empty = jnp.zeros((total_slots,) + values.shape[1:], values.dtype)
    return empty.at[target].set(values)


def relocate(packed, devices, slots_each):
    shaped = packed.reshape((devices, slots_each) + packed.shape[1:])
    arrived = lax.all_to_all(shaped, ("axial", "azim"), split_axis=0, concat_axis=0, tiled=True)
    return arrived.reshape((devices * slots_each,) + packed.shape[1:])


def shards(fields, new_owner, leaflet, stiffness, coarse, coarse_of_slot, viscosity):
    devices = lax.axis_size("axial") * lax.axis_size("azim")
    patch_count = fields.shape[0]
    slots_each = max(2, 3 * patch_count // (2 * devices))
    received = devices * slots_each
    owners = new_owner[:, 0]
    position = jnp.arange(patch_count)
    earlier = (owners[:, None] == owners[None, :]) & (position[None, :] < position[:, None])
    ranked = jnp.sum(earlier.astype(jnp.int32), axis=1)
    target = owners * slots_each + ranked
    sheets = leaflet_sheets(leaflet, stiffness)
    forced = fields + SPREAD * sheets.astype(jnp.float32)
    placed = relocate(place_slots(forced, target, received), devices, slots_each)
    strip_count = coarse.shape[0]
    onehot = (coarse_of_slot[:, None] == jnp.arange(strip_count)[None, :]).astype(jnp.float32)
    chosen = jnp.dot(onehot, coarse, precision=lax.Precision.HIGHEST).reshape(
        received, FIELDS, 2, PC // 2
    )
    interp = interp_table(PC // 2)
    ghosts = jnp.einsum("sfgk,kc->sfgc", chosen, interp, precision=lax.Precision.HIGHEST)
    row_count = fields.shape[2] // PC
    state = placed.reshape(received, FIELDS, row_count, PC)
    for sweep in range(STEPS):
        state = viscous(state, ghosts, viscosity)
    return state.reshape(received, FIELDS, row_count * PC)


def solution(mesh):
    placed = (
        P(("axial", "azim"), None, None),
        P(("axial", "azim"), None),
        P(None, "axial", "azim"),
        P(),
        P(("axial", "azim"), None),
        P(("axial", "azim")),
        P(),
    )
    return jax.shard_map(
        shards,
        mesh=mesh,
        in_specs=placed,
        out_specs=P(("axial", "azim"), None, None),
        check_vma=False,
    )
```

profile of v0, /device:TPU:0, one launch (start us, length us, event | category | flops | bytes accessed | tf_op | source)
XLA Modules:
  0.0 178.4 jit_solution(4914027032586986631)
XLA Ops:
  0.0 1.2 fusion.34
  1.2 5.0 %collective-permute-start = (bf16[64,1,256]{2,1,0:T(2,128)(2,1)S(1)}, bf16[64,1,256]{2,1,0:T(2,128)(2,1)S(1)}, u32[]{:S(2)}, u32[]{:S(2)}) collective-permute-start(bf16[64,1,256]{2,1,0:T(2,128)(2,1)S(1)} %get-tuple-element.5), channel_id=1, source_target_pairs={{0,8},{8,16},{16,24},{1,9},{9,17},{17,25},{2,10},{10,18},{18,26},{... | collective-permute-start | bytes 98312 | tf_op jit(solution)/shard_map/ppermute | solution.py:21
  6.1 1.3 collective-permute-start.1
  7.4 1.4 fusion.35
  8.9 2.6 %collective-permute-start.3 = (bf16[64,32,1]{2,1,0:T(8,128)(2,1)S(1)}, bf16[64,32,1]{2,1,0:T(8,128)(2,1)S(1)}, u32[]{:S(2)}, u32[]{:S(2)}) collective-permute-start(bf16[64,32,1]{2,1,0:T(8,128)(2,1)S(1)} %get-tuple-element.8), channel_id=1, source_target_pairs={{1,0},{2,1},{3,2},{4,3},{5,4},{6,5},{7,6},{0,7},{9,8},{10,9},{11,1... | collective-permute-start | bytes 12296 | tf_op jit(solution)/shard_map/ppermute | solution.py:22
  11.6 0.9 convert_reduce_fusion
  13.1 9.1 %collective-permute-done.2 = bf16[64,32,1]{2,1,0:T(8,128)(2,1)S(1)} collective-permute-done((bf16[64,32,1]{2,1,0:T(8,128)(2,1)S(1)}, bf16[64,32,1]{2,1,0:T(8,128)(2,1)S(1)}, u32[]{:S(2)}, u32[]{:S(2)}) %collective-permute-start.2) | collective-permute-done | bytes 4128 | tf_op jit(solution)/shard_map/ppermute | solution.py:21
  22.2 2.1 %maximum_convert_fusion = f32[64,32,258]{2,1,0:T(8,128)S(1)} fusion(bf16[64,32,1]{2,1,0:T(8,128)(2,1)S(1)} %collective-permute-done.3, bf16[64,32,256]{2,1,0:T(8,128)(2,1)} %param.9, bf16[64,32,1]{2,1,0:T(8,128)(2,1)S(1)} %collective-permute-done.2), kind=kLoop, calls=%fused_computation.26 | loop fusion | flops 3170304 | bytes 3170304 | tf_op jit(solution)/shard_map/convert_element_type | solution.py:57
  24.9 1.1 fusion.16
  27.1 4.2 %mul.66 = f32[64,32,4,64]{3,2,1,0:T(4,128)} reshape(f32[64,8192]{1,0:T(8,128)S(1)} %fusion.2) | data formatting | bytes 4194304 | tf_op jit(solution)/shard_map/mul | solution.py:95
  31.3 6.6 %copy.34 = f32[32,4,64,64]{3,2,1,0:T(8,128)} copy(f32[32,4,64,64]{3,1,0,2:T(4,128)} %bitcast.28) | data formatting | bytes 4194304 | tf_op jit(solution)/shard_map/mul | solution.py:95
  37.9 5.1 %mul.68 = f32[128,4,1024]{2,1,0:T(4,128)} reshape(f32[32,4,64,64]{3,2,1,0:T(8,128)} %copy.34) | data formatting | bytes 4194304 | tf_op jit(solution)/shard_map/mul | solution.py:95
  43.0 3.2 %add.90 = f32[128,4,1024]{2,1,0:T(4,128)S(1)} add(f32[128,4,1024]{2,1,0:T(4,128)} %param.7, f32[128,4,1024]{2,1,0:T(4,128)} %mul.68) | non-fusion elementwise | flops 524288 | bytes 6291456 | tf_op jit(solution)/shard_map/add | solution.py:95
  46.2 2.5 %broadcast_in_dim.2 = f32[192,4,1024]{2,1,0:T(4,128)} broadcast(f32[]{:T(128)} %constant.44.clone.1), dimensions={} | broadcast | bytes 3145732 | tf_op jit(solution)/shard_map/broadcast_in_dim | solution.py:74
  48.6 15.7 %scatter_fusion = f32[192,4,1024]{2,1,0:T(4,128)} fusion(f32[192,4,1024]{2,1,0:T(4,128)} %broadcast_in_dim.2, s32[128]{0:T(128)S(1)} %fusion.30, f32[128,4,1024]{2,1,0:T(4,128)S(1)} %add.90), kind=kCustom, calls=%fused_computation | custom fusion | bytes 6291968 | tf_op jit(solution)/shard_map/scatter | solution.py:75
  64.4 7.5 %all-to-all-start = ((f32[32,6,4,1024]{3,2,1,0:T(4,128)}), f32[32,6,4,1024]{3,2,1,0:T(4,128)S(1)}, u32[]{:S(2)}, u32[]{:S(2)}) async-start(f32[32,6,4,1024]{3,2,1,0:T(4,128)} %bitcast.5), calls=%async_computation | async-start | bytes 6291456 | tf_op jit(solution)/shard_map/all_to_all | solution.py:80
  73.6 1.8 %copy.37 = f32[192,4,1,64]{3,2,1,0:T(1,128)} copy(f32[192,4,1,64]{0,3,2,1:T(8,128)} %get-tuple-element.9) | data formatting | bytes 393216 | tf_op jit(solution)/shard_map/slice | solution.py:40
  75.4 1.0 copy.36
  76.4 66.7 %all-to-all-done = f32[32,6,4,1024]{3,2,1,0:T(4,128)S(1)} async-done(((f32[32,6,4,1024]{3,2,1,0:T(4,128)}), f32[32,6,4,1024]{3,2,1,0:T(4,128)S(1)}, u32[]{:S(2)}, u32[]{:S(2)}) %all-to-all-start) | async-done | bytes 3145760 | tf_op jit(solution)/shard_map/all_to_all | solution.py:80
  143.1 4.3 %reshape_reshape.3 = f32[192,4,16,64]{3,2,1,0:T(8,128)} reshape(f32[32,6,4,1024]{3,2,1,0:T(4,128)S(1)} %all-to-all-done) | data formatting | bytes 6291456 | tf_op jit(solution)/shard_map/reshape;reshape | solution.py:105
  147.4 12.9 %fusion.8 = f32[192,4,16,64]{3,2,1,0:T(8,128)S(1)} fusion(f32[192,4,16,64]{3,2,1,0:T(8,128)} %reshape_reshape.3, f32[192,4,1,64]{3,2,1,0:T(1,128)} %copy.36, f32[192,4,1,64]{3,2,1,0:T(1,128)} %copy.37, f32[4]{0:T(128)S(1)} %copy-done.5), kind=kLoop, calls=%fused_computation.14 | loop fusion | flops 7077888 | bytes 6684688 | tf_op jit(solution)/shard_map/add | solution.py:49
  160.3 6.5 %fusion.14 = f32[192,4,16,64]{3,2,1,0:T(8,128)} fusion(f32[192,4,16,64]{3,2,1,0:T(8,128)S(1)} %fusion.8, f32[192,4,1,64]{3,2,1,0:T(1,128)S(1)} %copy-done.3, f32[192,4,1,64]{3,2,1,0:T(1,128)S(1)} %copy-done.2, f32[4]{0:T(128)S(1)} %copy-done.5), kind=kLoop, calls=%fused_computation.20 | loop fusion | flops 7077888 | bytes 6684688 | tf_op jit(solution)/shard_map/add | solution.py:49
  166.8 6.7 %copy.40 = f32[192,4,16,64]{0,3,2,1:T(8,128)} copy(f32[192,4,16,64]{3,2,1,0:T(8,128)} %fusion.14) | data formatting | bytes 6291456 | tf_op jit(solution)/shard_map/add | solution.py:49
  173.4 4.9 %copy.41 = f32[192,4,1024]{2,1,0:T(4,128)} copy(f32[192,4,1024]{0,2,1:T(8,128)} %bitcast.27) | data formatting | bytes 6291456 | tf_op jit(solution)/shard_map/reshape | solution.py:108
  (26 shorter events, 4.1 us)
Async XLA Ops:
  0.0 71.8 %copy-start = (f32[64,256]{1,0:T(8,128)S(1)}, f32[64,256]{1,0:T(8,128)}, u32[]{:S(2)}) copy-start(f32[64,256]{1,0:T(8,128)} %param.11) | copy-start | bytes 196612
  1.2 23.1 %collective-permute-start = (bf16[64,1,256]{2,1,0:T(2,128)(2,1)S(1)}, bf16[64,1,256]{2,1,0:T(2,128)(2,1)S(1)}, u32[]{:S(2)}, u32[]{:S(2)}) collective-permute-start(bf16[64,1,256]{2,1,0:T(2,128)(2,1)S(1)} %get-tuple-element.5), channel_id=1, source_target_pairs={{0,8},{8,16},{16,24},{1,9},{9,17},{17,25},{2,10},{10,18},{18,26},{... | collective-permute-start | bytes 98312 | tf_op jit(solution)/shard_map/ppermute | solution.py:21
  6.1 18.2 %collective-permute-start.1 = (bf16[64,1,256]{2,1,0:T(2,128)(2,1)S(1)}, bf16[64,1,256]{2,1,0:T(2,128)(2,1)S(1)}, u32[]{:S(2)}, u32[]{:S(2)}) collective-permute-start(bf16[64,1,256]{2,1,0:T(2,128)(2,1)S(1)} %get-tuple-element.6), channel_id=1, source_target_pairs={{8,0},{16,8},{24,16},{9,1},{17,9},{25,17},{10,2},{18,10},{26,18},{... | collective-permute-start | bytes 98312 | tf_op jit(solution)/shard_map/ppermute | solution.py:22
  8.9 15.5 %copy-start.1 = (bf16[64,32,256]{2,1,0:T(8,128)(2,1)S(1)}, bf16[64,32,256]{2,1,0:T(8,128)(2,1)}, u32[]{:S(2)}) copy-start(bf16[64,32,256]{2,1,0:T(8,128)(2,1)} %param.9) | copy-start | bytes 3145732
  8.9 13.3 %collective-permute-start.2 = (bf16[64,32,1]{2,1,0:T(8,128)(2,1)S(1)}, bf16[64,32,1]{2,1,0:T(8,128)(2,1)S(1)}, u32[]{:S(2)}, u32[]{:S(2)}) collective-permute-start(bf16[64,32,1]{2,1,0:T(8,128)(2,1)S(1)} %get-tuple-element.7), channel_id=1, source_target_pairs={{0,1},{1,2},{2,3},{3,4},{4,5},{5,6},{6,7},{7,0},{8,9},{9,10},{10,1... | collective-permute-start | bytes 12296 | tf_op jit(solution)/shard_map/ppermute | solution.py:21
  8.9 13.3 %collective-permute-start.3 = (bf16[64,32,1]{2,1,0:T(8,128)(2,1)S(1)}, bf16[64,32,1]{2,1,0:T(8,128)(2,1)S(1)}, u32[]{:S(2)}, u32[]{:S(2)}) collective-permute-start(bf16[64,32,1]{2,1,0:T(8,128)(2,1)S(1)} %get-tuple-element.8), channel_id=1, source_target_pairs={{1,0},{2,1},{3,2},{4,3},{5,4},{6,5},{7,6},{0,7},{9,8},{10,9},{11,1... | collective-permute-start | bytes 12296 | tf_op jit(solution)/shard_map/ppermute | solution.py:22
  24.9 1.8 %copy-start.4 = (bf16[64,64]{1,0:T(8,128)(2,1)S(1)}, bf16[64,64]{1,0:T(8,128)(2,1)}, u32[]{:S(2)}) copy-start(bf16[64,64]{1,0:T(8,128)(2,1)} %param.10) | copy-start | bytes 24580
  64.4 7.5 %copy-start.6 = (s32[192]{0:T(256)S(1)}, s32[192]{0:T(256)}, u32[]{:S(2)}) copy-start(s32[192]{0:T(256)} %param.12) | copy-start | bytes 2308
  64.4 78.7 %all-to-all-start = ((f32[32,6,4,1024]{3,2,1,0:T(4,128)}), f32[32,6,4,1024]{3,2,1,0:T(4,128)S(1)}, u32[]{:S(2)}, u32[]{:S(2)}) async-start(f32[32,6,4,1024]{3,2,1,0:T(4,128)} %bitcast.5), calls=%async_computation | async-start | bytes 6291456 | tf_op jit(solution)/shard_map/all_to_all | solution.py:80
  76.4 71.0 %copy-start.5 = (f32[4]{0:T(128)S(1)}, f32[4]{0:T(128)}, u32[]{:S(2)}) copy-start(f32[4]{0:T(128)} %param.13) | copy-start | bytes 52
  147.4 12.9 %copy-start.2 = (f32[192,4,1,64]{3,2,1,0:T(1,128)S(1)}, f32[192,4,1,64]{3,2,1,0:T(1,128)}, u32[]{:S(2)}) copy-start(f32[192,4,1,64]{3,2,1,0:T(1,128)} %copy.37) | copy-start | bytes 589828
  147.4 12.9 %copy-start.3 = (f32[192,4,1,64]{3,2,1,0:T(1,128)S(1)}, f32[192,4,1,64]{3,2,1,0:T(1,128)}, u32[]{:S(2)}) copy-start(f32[192,4,1,64]{3,2,1,0:T(1,128)} %copy.36) | copy-start | bytes 589828
where the time goes:
time: 179 us; the launch traced here: 178 us
  waiting for transfers between devices  75.8 us (42%)
  local copies, waits for them, and re-layouts  56.8 us (32%)
  other arithmetic  27.9 us (16%)
  starting transfers between devices  16.4 us (9%)
    all_to_all x1, waiting for transfers between devices, relocate(): lax.all_to_all(shaped, ('axial', 'azim'), split_axis=0, concat_axis=0, ti...  66.7 us
    add x2, other arithmetic, viscous(): return state + viscosity[None, :, None, None] * laplace  19.4 us
    mul x3, local copies, waits for them, and re-layouts, shards(): forced = fields + SPREAD * sheets.astype(jnp.float32)  15.9 us
    scatter x1, local copies, waits for them, and re-layouts, place_slots(): return empty.at[target].set(values)  15.7 us
    ppermute x2, waiting for transfers between devices, padded(): before = lax.ppermute(last, axis, up)  9.06 us
    all_to_all x1, starting transfers between devices, relocate(): lax.all_to_all(shaped, ('axial', 'azim'), split_axis=0, concat_axis=0, ti...  7.46 us
    add x1, local copies, waits for them, and re-layouts, viscous(): return state + viscosity[None, :, None, None] * laplace  6.69 us
    ppermute x2, starting transfers between devices, padded(): before = lax.ppermute(last, axis, up)  5.02 us
  transfers between devices with their start and end apart: 5, of which 2 were waited for; matrix products, arithmetic and copies ran while one was open for 5% of the time, Pallas kernels for 0%

commit v1 on v0

v1 whole, which is shorter than its diff:
```python
import functools
import jax
import jax.numpy as jnp
from jax import lax
from jax.experimental import pallas as pl
from jax.experimental.pallas import tpu as pltpu
from jax.sharding import PartitionSpec as P

PC = 64
FIELDS = 4
STEPS = 2
SPREAD = 0.25
LANES = 128
MESH = pl.DeviceIdType.MESH
F32 = jnp.float32
BF16 = jnp.bfloat16


def iota(shape, dim):
    return lax.broadcasted_iota(jnp.int32, shape, dim)


def peers(n_ax, n_az):
    half = n_ax // 2
    near = sorted(range(n_ax), key=lambda d: abs(d - half))
    return [(da, dz) for da in near for dz in range(n_az) if (da, dz) != (0, 0)]


def send_kernel(
    n_ax, n_az, each, pick_ref, fields_ref, leaf_ref, stiff_ref, out_ref,
    rows_f, cols_f, edge_rows, edge_cols, got_rows, got_cols, lap_ref, forced_ref, packed_ref,
    halo_send, halo_recv, send_sem, recv_sem,
):
    a = lax.axis_index("axial")
    z = lax.axis_index("azim")
    me = a * n_az + z
    records, rows, cols = leaf_ref.shape
    patches = fields_ref.shape[0]
    blocks = rows // 8
    order = peers(n_ax, n_az)

    got_rows[...] = jnp.zeros_like(got_rows)
    barrier = pltpu.get_barrier_semaphore()
    for da, dz in order:
        pl.semaphore_signal(
            barrier, inc=1,
            device_id=(lax.rem(a + da, n_ax), lax.rem(z + dz, n_az)), device_id_type=MESH,
        )

    row_id = iota((rows, LANES), 0)
    lane_id = iota((rows, LANES), 1)
    eye_low = lane_id == row_id
    eye_high = lane_id == row_id + rows

    def edges(k, carry):
        x = leaf_ref[k].astype(F32)
        rows_f[0, pl.ds(k, 1), :] = x[0:1, :]
        rows_f[1, pl.ds(k, 1), :] = x[rows - 1:rows, :]
        first = jnp.broadcast_to(x[:, 0:1], (rows, LANES))
        last = jnp.broadcast_to(x[:, cols - 1:cols], (rows, LANES))
        both = jnp.where(eye_low, first, jnp.where(eye_high, last, 0.0))
        cols_f[pl.ds(k, 1), :] = jnp.sum(both, axis=0, keepdims=True)
        return carry

    lax.fori_loop(0, records, edges, 0, unroll=4)
    edge_rows[...] = rows_f[...].astype(BF16)
    edge_cols[...] = cols_f[...].astype(BF16)
    pl.semaphore_wait(barrier, len(order))

    def halo(src, dst, i, device):
        return pltpu.make_async_remote_copy(
            src_ref=src, dst_ref=dst, send_sem=halo_send.at[i], recv_sem=halo_recv.at[i],
            device_id=device, device_id_type=MESH,
        )

    down = halo(edge_rows.at[1], got_rows.at[0], 0, (lax.rem(a + 1, n_ax), z))
    up = halo(edge_rows.at[0], got_rows.at[1], 1, (lax.rem(a + n_ax - 1, n_ax), z))
    right = halo(edge_cols, got_cols.at[0], 2, (a, lax.rem(z + 1, n_az)))
    left = halo(edge_cols, got_cols.at[1], 3, (a, lax.rem(z + n_az - 1, n_az)))

    @pl.when(a < n_ax - 1)
    def _():
        down.start()

    @pl.when(a > 0)
    def _():
        up.start()

    right.start()
    left.start()

    pairs = records // FIELDS // 2
    width = pairs * FIELDS
    big = 8 * records
    out_row = iota((big, records), 0)
    record = iota((big, records), 1)
    within = lax.rem(out_row, width)
    wanted = lax.rem(within, FIELDS) * (2 * pairs) + 2 * (within // FIELDS) + out_row // (8 * width)
    row_pick = (record == wanted).astype(BF16)
    col_pick = (iota((records, big), 0) == iota((records, big), 1) // 8).astype(BF16)
    spread = jnp.dot(stiff_ref[...], col_pick, preferred_element_type=F32).astype(BF16)
    spread = jnp.dot(row_pick, spread, preferred_element_type=F32)
    same = lax.rem(iota((big, big), 0) // width, 8) == lax.rem(iota((big, big), 1), 8)
    law = jnp.where(same, spread, 0.0).astype(BF16)
    forced_ref[patches] = jnp.zeros(forced_ref.shape[1:], BF16)

    @pl.when(a > 0)
    def _():
        down.wait_recv()

    @pl.when(a < n_ax - 1)
    def _():
        up.wait_recv()

    right.wait_recv()
    left.wait_recv()
    rows_f2 = got_rows[...].astype(F32)
    cols_l = got_cols[0].astype(F32)
    cols_r = got_cols[1].astype(F32)

    @pl.when(a < n_ax - 1)
    def _():
        down.wait_send()

    @pl.when(a > 0)
    def _():
        up.wait_send()

    right.wait_send()
    left.wait_send()
    rows_f[...] = rows_f2
    cols_f[...] = jnp.where(iota(cols_l.shape, 1) < rows, cols_r, cols_l)
    wide_row = iota((rows, cols), 0)
    wide_lane = iota((rows, cols), 1)

    def laplace(k, carry):
        x = leaf_ref[k].astype(F32)
        halo_cols = jnp.broadcast_to(cols_f[pl.ds(k, 1), :], (rows, LANES))
        after = jnp.sum(jnp.where(eye_low, halo_cols, 0.0), axis=1, keepdims=True)
        before = jnp.sum(jnp.where(eye_high, halo_cols, 0.0), axis=1, keepdims=True)
        north = jnp.where(wide_row == 0, rows_f[0, pl.ds(k, 1), :], pltpu.roll(x, 1, 0))
        south = jnp.where(wide_row == rows - 1, rows_f[1, pl.ds(k, 1), :], pltpu.roll(x, rows - 1, 0))
        west = jnp.where(wide_lane == 0, before, pltpu.roll(x, 1, 1))
        east = jnp.where(wide_lane == cols - 1, after, pltpu.roll(x, cols - 1, 1))
        total = south + north + west + east - 4.0 * x
        for b in range(blocks):
            lap_ref[b, pl.ds(pl.multiple_of(k * 8, 8), 8), :] = total[b * 8:(b + 1) * 8, :]
        return carry

    lax.fori_loop(0, records, laplace, 0, unroll=4)

    low = iota((width, LANES), 1) < PC
    across = cols // PC

    def force(b, carry):
        tension = jnp.dot(law, lap_ref[b].astype(BF16), preferred_element_type=F32)
        tension = tension.astype(BF16).astype(F32) * SPREAD
        for r in range(8):
            for t in range(cols // LANES):
                even = tension[r * width:(r + 1) * width, t * LANES:(t + 1) * LANES]
                odd = tension[(8 + r) * width:(9 + r) * width, t * LANES:(t + 1) * LANES]
                p = (b * 8 + r) * across + 2 * t
                first = jnp.where(low, even, pltpu.roll(odd, PC, 1))
                second = jnp.where(low, pltpu.roll(even, PC, 1), odd)
                forced_ref[p] = (fields_ref[p] + first).astype(BF16)
                forced_ref[p + 1] = (fields_ref[p + 1] + second).astype(BF16)
        return carry

    lax.fori_loop(0, blocks, force, 0)

    copies = []
    for i, (da, dz) in enumerate(order):
        ta, tz = lax.rem(a + da, n_ax), lax.rem(z + dz, n_az)
        other = ta * n_az + tz
        for k in range(each):
            packed_ref[other, k] = forced_ref[pick_ref[other * each + k]]
        copy = pltpu.make_async_remote_copy(
            src_ref=packed_ref.at[other], dst_ref=out_ref.at[me],
            send_sem=send_sem.at[i], recv_sem=recv_sem.at[i],
            device_id=(ta, tz), device_id_type=MESH,
        )
        copy.start()
        copies.append(copy)
    for k in range(each):
        out_ref[me, k] = forced_ref[pick_ref[me * each + k]]
    for i, (da, dz) in enumerate(order):
        source = lax.rem(a + n_ax - da, n_ax) * n_az + lax.rem(z + n_az - dz, n_az)
        pltpu.make_async_remote_copy(
            src_ref=packed_ref.at[source], dst_ref=out_ref.at[source],
            send_sem=send_sem.at[i], recv_sem=recv_sem.at[i],
            device_id=(a, z), device_id_type=MESH,
        ).wait_recv()
    for copy in copies:
        copy.wait_send()


def step_slots(state, ghost, nu):
    slots, height, lanes = state.shape
    shape = (slots, height, lanes)
    lane = iota(shape, 2)
    row = iota(shape, 1)
    cell = lax.rem(lane, PC)
    flat = slots * height
    for _ in range(STEPS):
        wide = state.reshape(flat, lanes)
        swap = pltpu.roll(wide, PC, 1).reshape(shape)
        west = jnp.where(cell == 0, 0.0, pltpu.roll(wide, 1, 1).reshape(shape))
        east = jnp.where(cell == PC - 1, 0.0, pltpu.roll(wide, lanes - 1, 1).reshape(shape))
        above = jnp.concatenate([ghost, swap[:, :height - FIELDS]], axis=1)
        below = jnp.concatenate([swap[:, FIELDS:], ghost], axis=1)
        total = swap + jnp.where(lane < PC, above, below) + west + east - 4.0 * state
        state = state + nu * total
    return state


def relax_kernel(group, idx_ref, coarse_ref, nu_ref, in_ref, out_ref, ghost_ref):
    @pl.when(pl.program_id(0) == 0)
    def _():
        strips = coarse_ref.shape[0]
        fine = iota((PC, LANES), 1)
        src = iota((PC, LANES), 0)
        half = PC // 2
        near = (fine // PC) * half + lax.rem(fine, PC) // 2
        cell = lax.rem(fine, PC)
        second = jnp.where(
            lax.rem(fine, 2) == 0,
            jnp.where(cell == 0, near, near - 1),
            jnp.where(cell == PC - 1, near, near + 1),
        )
        table = (0.75 * (src == near).astype(F32) + 0.25 * (src == second).astype(F32)).astype(BF16)
        hot = (idx_ref[...] == iota((idx_ref.shape[0], FIELDS * strips), 1)).astype(BF16)
        parts = []
        for f in range(FIELDS):
            raw = coarse_ref[:, f * PC:(f + 1) * PC]
            top = raw.astype(BF16)
            rest = (raw - top.astype(F32)).astype(BF16)
            parts.append(
                jnp.dot(top, table, preferred_element_type=F32)
                + jnp.dot(rest, table, preferred_element_type=F32)
            )
        strip = jnp.concatenate(parts, axis=0)
        top = strip.astype(BF16)
        rest = (strip - top.astype(F32)).astype(BF16)
        ghost = jnp.dot(hot, top, preferred_element_type=F32)
        ghost = ghost + jnp.dot(hot, rest, preferred_element_type=F32)
        ghost_ref[...] = ghost.reshape(ghost_ref.shape)

    base = pl.program_id(0) * group
    for s in range(group):
        ghost = ghost_ref[base + s][None, :FIELDS]
        out_ref[s] = step_slots(in_ref[s].astype(F32)[None], ghost, nu_ref[...][None])[0]


def shards(mesh, fields, new_owner, leaflet, stiffness, coarse, coarse_of_slot, viscosity):
    n_ax, n_az = mesh.shape["axial"], mesh.shape["azim"]
    devices = n_ax * n_az
    patches, _, section = fields.shape
    records = leaflet.shape[0]
    each = max(2, 3 * patches // (2 * devices))
    slots = devices * each
    owners = new_owner[:, 0]
    place = jnp.arange(patches)
    earlier = (owners[:, None] == owners[None, :]) & (place[None, :] < place[:, None])
    target = owners * each + jnp.sum(earlier.astype(jnp.int32), axis=1)
    taken = target[None, :] == jnp.arange(slots)[:, None]
    pick = patches + jnp.sum(jnp.where(taken, place[None, :] - patches, 0), axis=1)
    height = FIELDS * section // LANES
    view = fields.reshape(patches, FIELDS, section // LANES, LANES).transpose(0, 2, 1, 3)
    view = view.reshape(patches, height, LANES)
    rows, cols = leaflet.shape[1:]
    vmem = pl.BlockSpec(memory_space=pltpu.VMEM)
    moved = pl.pallas_call(
        functools.partial(send_kernel, n_ax, n_az, each),
        out_shape=jax.ShapeDtypeStruct((devices, each, height, LANES), BF16),
        in_specs=[pl.BlockSpec(memory_space=pltpu.SMEM), vmem, vmem, vmem],
        out_specs=vmem,
        scratch_shapes=[
            pltpu.VMEM((2, records, cols), F32),
            pltpu.VMEM((records, LANES), F32),
            pltpu.VMEM((2, records, cols), BF16),
            pltpu.VMEM((records, LANES), BF16),
            pltpu.VMEM((2, records, cols), BF16),
            pltpu.VMEM((2, records, LANES), BF16),
            pltpu.VMEM((rows // 8, 8 * records, cols), F32),
            pltpu.VMEM((patches + 1, height, LANES), BF16),
            pltpu.VMEM((devices, each, height, LANES), BF16),
            pltpu.SemaphoreType.DMA((4,)),
            pltpu.SemaphoreType.DMA((4,)),
            pltpu.SemaphoreType.DMA((devices - 1,)),
            pltpu.SemaphoreType.DMA((devices - 1,)),
        ],
        compiler_params=pltpu.CompilerParams(collective_id=0, has_side_effects=True),
        name="send",
    )(pick, view, leaflet, stiffness)

    group = 16
    index = coarse_of_slot[:, None] + coarse.shape[0] * (jnp.arange(2 * FIELDS) % FIELDS)[None, :]
    nu = jnp.broadcast_to(jnp.tile(viscosity, height // FIELDS)[:, None], (height, LANES))
    whole = lambda shape: pl.BlockSpec(shape, lambda i: (0,) * len(shape))
    out = pl.pallas_call(
        functools.partial(relax_kernel, group),
        grid=(slots // group,),
        out_shape=jax.ShapeDtypeStruct((slots, height, LANES), F32),
        in_specs=[
            whole((slots * 2 * FIELDS, 1)), whole(coarse.shape), whole((height, LANES)),
            pl.BlockSpec((group, height, LANES), lambda i: (i, 0, 0)),
        ],
        out_specs=pl.BlockSpec((group, height, LANES), lambda i: (i, 0, 0)),
        scratch_shapes=[pltpu.VMEM((slots, 2 * FIELDS, LANES), F32)],
        name="relax",
    )(index.reshape(-1, 1), coarse, nu, moved.reshape(slots, height, LANES))
    out = out.reshape(slots, section // LANES, FIELDS, LANES).transpose(0, 2, 1, 3)
    return out.reshape(slots, FIELDS, section)


def solution(mesh):
    placed = (
        P(("axial", "azim"), None, None),
        P(("axial", "azim"), None),
        P(None, "axial", "azim"),
        P(),
        P(("axial", "azim"), None),
        P(("axial", "azim")),
        P(),
    )
    return jax.shard_map(
        functools.partial(shards, mesh),
        mesh=mesh,
        in_specs=placed,
        out_specs=P(("axial", "azim"), None, None),
        check_vma=False,
    )
```

time: 179 us -> 74.2 us (0.41)
  the two profiles are of different devices: /device:TPU:0 before, /device:TPU:17 now
where the time goes in v1:
time: 74.2 us; the launch traced here: 73.8 us
  Pallas kernels  68.2 us (92%)
  other arithmetic  3.01 us (4%)
  local copies, waits for them, and re-layouts  2.55 us (3%)
    pallas_call x1, Pallas kernels, shards(): pl.pallas_call(functools.partial(send_kernel, n_ax, n_az, each), out_shap...  51.5 us
    pallas_call x1, Pallas kernels, shards(): pl.pallas_call(functools.partial(relax_kernel, group), grid=(slots // gro...  16.7 us

profile of v1, /device:TPU:17, one launch (start us, length us, event | category | flops | bytes accessed | tf_op | source)
XLA Modules:
  0.0 73.8 jit_solution(17907257769429295942)
XLA Ops:
  0.0 0.9 %convert_reduce_fusion = s32[128]{0:T(128)S(1)} fusion(s32[128]{0:T(128)} %bitcast.15), kind=kLoop, calls=%fused_computation.2 | loop fusion | flops 81792 | bytes 1024 | tf_op jit(solution)/shard_map/reduce_sum | solution.py:264
  0.9 0.7 iota_add_fusion
  1.6 0.1 select_reduce_fusion
  1.7 0.6 broadcast_add_fusion.1.pick_ref
  2.3 0.7 tile.2
  2.9 0.1 broadcast_in_dim.16
  3.0 0.7 broadcast_in_dim.17.nu_ref
  3.7 0.8 %broadcast_add_fusion = s32[192,8]{1,0:T(8,128)S(1)} fusion(s32[8]{0:T(128)S(1)} %fusion.1, s32[192]{0:T(256)} %param.12), kind=kLoop, calls=%fused_computation.5 | loop fusion | flops 1536 | bytes 6944 | tf_op jit(solution)/shard_map/add | solution.py:297
  4.4 1.1 %add.60.idx_ref = s32[1536,1]{1,0:T(8,128)} reshape(s32[192,8]{1,0:T(8,128)S(1)} %broadcast_add_fusion) | data formatting | bytes 12288 | tf_op jit(solution)/shard_map/add | solution.py:297
  5.6 51.5 %send.1 = bf16[32,6,32,128]{3,2,1,0:T(8,128)(2,1)} custom-call(s32[192]{0:T(256)} %broadcast_add_fusion.1.pick_ref, f32[128,32,128]{2,1,0:T(8,128)} %bitcast.14, bf16[64,32,256]{2,1,0:T(8,128)(2,1)} %leaf_ref.1, bf16[64,64]{1,0:T(8,128)(2,1)} %stiff_ref.1), custom_call_target="tpu_custom_call" | custom-call | tf_op jit(solution)/shard_map/send/pallas_call | solution.py:272
  57.1 16.7 %relax.1 = f32[192,32,128]{2,1,0:T(8,128)} custom-call(s32[1536,1]{1,0:T(8,128)} %add.60.idx_ref, f32[64,256]{1,0:T(8,128)} %coarse_ref.1, f32[32,128]{1,0:T(8,128)} %broadcast_in_dim.17.nu_ref, bf16[192,32,128]{2,1,0:T(8,128)(2,1)} %bitcast.13), custom_call_target="tpu_custom_call" | custom-call | tf_op jit(solution)/shard_map/relax/pallas_call | solution.py:300
  (1 shorter events, 0.0 us)

commit v2 on v1

v2 whole, which is shorter than its diff:
```python
import functools
import jax
import jax.numpy as jnp
from jax import lax
from jax.experimental import pallas as pl
from jax.experimental.pallas import tpu as pltpu
from jax.sharding import PartitionSpec as P

PC = 64
FIELDS = 4
STEPS = 2
SPREAD = 0.25
LANES = 128
MESH = pl.DeviceIdType.MESH
F32 = jnp.float32
BF16 = jnp.bfloat16


def iota(shape, dim):
    return lax.broadcasted_iota(jnp.int32, shape, dim)


def peer(i, n_ax, n_az):
    j = i // n_az
    da = lax.rem(n_ax // 2 + ((j + 1) // 2) * (1 - 2 * lax.rem(j, 2)), n_ax)
    return da, lax.rem(lax.rem(i, n_az) + 1, n_az)


def send_kernel(
    n_ax, n_az, each, owner_ref, slot_ref, nu_ref, fields_ref, leaf_ref, stiff_ref, coarse_ref, out_ref,
    rows_f, cols_f, edge_rows, edge_cols, got_rows, got_cols, lap_ref, forced_ref, packed_ref,
    landed_ref, done_ref, strip_ref, pick_row, pick_ref,
    halo_send, halo_recv, send_sem, recv_sem, out_sem, pick_sem,
):
    a = lax.axis_index("axial")
    z = lax.axis_index("azim")
    me = a * n_az + z
    devices = n_ax * n_az
    records, rows, cols = leaf_ref.shape
    patches, height, _ = fields_ref.shape
    blocks = rows // 8

    got_rows[...] = jnp.zeros_like(got_rows)
    barrier = pltpu.get_barrier_semaphore()

    def greet(i, carry):
        da, dz = peer(i, n_ax, n_az)
        pl.semaphore_signal(
            barrier, inc=1,
            device_id=(lax.rem(a + da, n_ax), lax.rem(z + dz, n_az)), device_id_type=MESH,
        )
        return carry

    lax.fori_loop(0, devices - 1, greet, 0)

    row_id = iota((rows, LANES), 0)
    lane_id = iota((rows, LANES), 1)
    eye_low = lane_id == row_id
    eye_high = lane_id == row_id + rows

    def edges(k, carry):
        x = leaf_ref[k].astype(F32)
        rows_f[0, pl.ds(k, 1), :] = x[0:1, :]
        rows_f[1, pl.ds(k, 1), :] = x[rows - 1:rows, :]
        first = jnp.broadcast_to(x[:, 0:1], (rows, LANES))
        last = jnp.broadcast_to(x[:, cols - 1:cols], (rows, LANES))
        both = jnp.where(eye_low, first, jnp.where(eye_high, last, 0.0))
        cols_f[pl.ds(k, 1), :] = jnp.sum(both, axis=0, keepdims=True)
        return carry

    lax.fori_loop(0, records, edges, 0, unroll=4)
    edge_rows[...] = rows_f[...].astype(BF16)
    edge_cols[...] = cols_f[...].astype(BF16)
    pl.semaphore_wait(barrier, devices - 1)

    def halo(src, dst, i, device):
        return pltpu.make_async_remote_copy(
            src_ref=src, dst_ref=dst, send_sem=halo_send.at[i], recv_sem=halo_recv.at[i],
            device_id=device, device_id_type=MESH,
        )

    down = halo(edge_rows.at[1], got_rows.at[0], 0, (lax.rem(a + 1, n_ax), z))
    up = halo(edge_rows.at[0], got_rows.at[1], 1, (lax.rem(a + n_ax - 1, n_ax), z))
    right = halo(edge_cols, got_cols.at[0], 2, (a, lax.rem(z + 1, n_az)))
    left = halo(edge_cols, got_cols.at[1], 3, (a, lax.rem(z + n_az - 1, n_az)))

    @pl.when(a < n_ax - 1)
    def _():
        down.start()

    @pl.when(a > 0)
    def _():
        up.start()

    right.start()
    left.start()

    pairs = records // FIELDS // 2
    width = pairs * FIELDS
    big = 8 * records
    out_row = iota((big, records), 0)
    record = iota((big, records), 1)
    within = lax.rem(out_row, width)
    wanted = lax.rem(within, FIELDS) * (2 * pairs) + 2 * (within // FIELDS) + out_row // (8 * width)
    row_pick = (record == wanted).astype(BF16)
    col_pick = (iota((records, big), 0) == iota((records, big), 1) // 8).astype(BF16)
    spread = jnp.dot(stiff_ref[...], col_pick, preferred_element_type=F32).astype(BF16)
    spread = jnp.dot(row_pick, spread, preferred_element_type=F32)
    same = lax.rem(iota((big, big), 0) // width, 8) == lax.rem(iota((big, big), 1), 8)
    law = jnp.where(same, spread, 0.0).astype(BF16)
    forced_ref[patches] = jnp.zeros(forced_ref.shape[1:], BF16)
    pick_slots(each, owner_ref, pick_row)
    picked = pltpu.make_async_copy(pick_row, pick_ref, pick_sem)
    picked.start()
    interpolate(coarse_ref, strip_ref)

    @pl.when(a > 0)
    def _():
        down.wait_recv()

    @pl.when(a < n_ax - 1)
    def _():
        up.wait_recv()

    right.wait_recv()
    left.wait_recv()
    rows_f2 = got_rows[...].astype(F32)
    cols_l = got_cols[0].astype(F32)
    cols_r = got_cols[1].astype(F32)

    @pl.when(a < n_ax - 1)
    def _():
        down.wait_send()

    @pl.when(a > 0)
    def _():
        up.wait_send()

    right.wait_send()
    left.wait_send()
    rows_f[...] = rows_f2
    cols_f[...] = jnp.where(iota(cols_l.shape, 1) < rows, cols_r, cols_l)
    wide_row = iota((rows, cols), 0)
    wide_lane = iota((rows, cols), 1)

    def laplace(k, carry):
        x = leaf_ref[k].astype(F32)
        halo_cols = jnp.broadcast_to(cols_f[pl.ds(k, 1), :], (rows, LANES))
        after = jnp.sum(jnp.where(eye_low, halo_cols, 0.0), axis=1, keepdims=True)
        before = jnp.sum(jnp.where(eye_high, halo_cols, 0.0), axis=1, keepdims=True)
        north = jnp.where(wide_row == 0, rows_f[0, pl.ds(k, 1), :], pltpu.roll(x, 1, 0))
        south = jnp.where(wide_row == rows - 1, rows_f[1, pl.ds(k, 1), :], pltpu.roll(x, rows - 1, 0))
        west = jnp.where(wide_lane == 0, before, pltpu.roll(x, 1, 1))
        east = jnp.where(wide_lane == cols - 1, after, pltpu.roll(x, cols - 1, 1))
        total = south + north + west + east - 4.0 * x
        for b in range(blocks):
            lap_ref[b, pl.ds(pl.multiple_of(k * 8, 8), 8), :] = total[b * 8:(b + 1) * 8, :]
        return carry

    lax.fori_loop(0, records, laplace, 0, unroll=4)

    low = iota((width, LANES), 1) < PC
    across = cols // PC

    def force(b, carry):
        tension = jnp.dot(law, lap_ref[b].astype(BF16), preferred_element_type=F32)
        tension = tension.astype(BF16).astype(F32) * SPREAD
        for r in range(8):
            for t in range(cols // LANES):
                even = tension[r * width:(r + 1) * width, t * LANES:(t + 1) * LANES]
                odd = tension[(8 + r) * width:(9 + r) * width, t * LANES:(t + 1) * LANES]
                p = (b * 8 + r) * across + 2 * t
                first = jnp.where(low, even, pltpu.roll(odd, PC, 1))
                second = jnp.where(low, pltpu.roll(even, PC, 1), odd)
                forced_ref[p] = (fields_ref[p] + first).astype(BF16)
                forced_ref[p + 1] = (fields_ref[p + 1] + second).astype(BF16)
        return carry

    lax.fori_loop(0, blocks, force, 0)

    picked.wait()

    def outgoing(i):
        da, dz = peer(i, n_ax, n_az)
        ta, tz = lax.rem(a + da, n_ax), lax.rem(z + dz, n_az)
        other = ta * n_az + tz
        return other, pltpu.make_async_remote_copy(
            src_ref=packed_ref.at[other], dst_ref=landed_ref.at[me],
            send_sem=send_sem.at[i], recv_sem=recv_sem.at[i],
            device_id=(ta, tz), device_id_type=MESH,
        )

    def send(i, carry):
        other, copy = outgoing(i)
        for k in range(each):
            packed_ref[other, k] = forced_ref[pick_ref[0, other * each + k]]
        copy.start()
        return carry

    lax.fori_loop(0, devices - 1, send, 0)

    row = iota((height, LANES), 0)
    nu = jnp.full((height, LANES), nu_ref[0], F32)
    for f in range(1, FIELDS):
        nu = jnp.where(lax.rem(row, FIELDS) == f, nu_ref[f], nu)

    def written(source):
        return pltpu.make_async_copy(done_ref.at[source], out_ref.at[source], out_sem.at[source])

    for k in range(each):
        ghost = strip_ref[slot_ref[me * each + k]]
        block = forced_ref[pick_ref[0, me * each + k]].astype(F32)
        done_ref[me, k] = relax(block, ghost, nu)
    written(me).start()

    def arrive(i, carry):
        da, dz = peer(i, n_ax, n_az)
        source = lax.rem(a + n_ax - da, n_ax) * n_az + lax.rem(z + n_az - dz, n_az)
        pltpu.make_async_remote_copy(
            src_ref=packed_ref.at[source], dst_ref=landed_ref.at[source],
            send_sem=send_sem.at[i], recv_sem=recv_sem.at[i],
            device_id=(a, z), device_id_type=MESH,
        ).wait_recv()
        for k in range(each):
            ghost = strip_ref[slot_ref[source * each + k]]
            done_ref[source, k] = relax(landed_ref[source, k].astype(F32), ghost, nu)
        written(source).start()
        return carry

    lax.fori_loop(0, devices - 1, arrive, 0)

    def finish(i, carry):
        outgoing(i)[1].wait_send()
        written(i).wait()
        return carry

    lax.fori_loop(0, devices - 1, finish, 0)
    written(devices - 1).wait()


def pick_slots(each, owner_ref, pick_row):
    patches = owner_ref.shape[1]
    slots = pick_row.shape[1]
    square = (patches, patches)
    eye = iota(square, 0) == iota(square, 1)
    owner = owner_ref[...]
    across = jnp.broadcast_to(owner, square)
    along = jnp.sum(jnp.where(eye, across, 0), axis=1, keepdims=True)
    earlier = (along == across) & (iota(square, 0) < iota(square, 1))
    rank = jnp.sum(earlier.astype(jnp.int32), axis=0, keepdims=True)
    target = jnp.broadcast_to(owner * each + rank, square)
    target = jnp.sum(jnp.where(eye, target, 0), axis=1, keepdims=True)
    shape = (patches, slots)
    taken = target == iota(shape, 1)
    pick_row[...] = patches + jnp.sum(
        jnp.where(taken, iota(shape, 0) - patches, 0), axis=0, keepdims=True
    )


def interpolate(coarse_ref, strip_ref):
    fine = iota((PC, LANES), 1)
    src = iota((PC, LANES), 0)
    cell = lax.rem(fine, PC)
    near = (fine // PC) * (PC // 2) + cell // 2
    second = jnp.where(
        lax.rem(fine, 2) == 0,
        jnp.where(cell == 0, near, near - 1),
        jnp.where(cell == PC - 1, near, near + 1),
    )
    table = (0.75 * (src == near).astype(F32) + 0.25 * (src == second).astype(F32)).astype(BF16)
    for f in range(FIELDS):
        raw = coarse_ref[:, f * PC:(f + 1) * PC]
        top = raw.astype(BF16)
        rest = (raw - top.astype(F32)).astype(BF16)
        fine_cells = jnp.dot(top, table, preferred_element_type=F32)
        fine_cells = fine_cells + jnp.dot(rest, table, preferred_element_type=F32)
        strip_ref[:, f, :] = fine_cells
        strip_ref[:, FIELDS + f, :] = fine_cells


def relax(state, ghost, nu):
    shape = (8, LANES)
    lane = iota(shape, 1)
    low = iota(shape, 0) < FIELDS
    cell = lax.rem(lane, PC)
    up = (lane < PC) & low
    down = (lane >= PC) & (iota(shape, 0) >= FIELDS)
    count = state.shape[0] // 8
    tiles = [state[8 * j:8 * j + 8] for j in range(count)]
    for _ in range(STEPS):
        swap = [pltpu.roll(t, PC, 1) for t in tiles]
        turned = [ghost] + [pltpu.roll(t, FIELDS, 0) for t in swap] + [ghost]
        fresh = []
        for j, t in enumerate(tiles):
            beyond = jnp.where(up, turned[j], jnp.where(down, turned[j + 2], turned[j + 1]))
            west = jnp.where(cell == 0, 0.0, pltpu.roll(t, 1, 1))
            east = jnp.where(cell == PC - 1, 0.0, pltpu.roll(t, LANES - 1, 1))
            total = swap[j] + beyond + west + east - 4.0 * t
            fresh.append(t + nu[8 * j:8 * j + 8] * total)
        tiles = fresh
    return jnp.concatenate(tiles, axis=0)


def shards(mesh, fields, new_owner, leaflet, stiffness, coarse, coarse_of_slot, viscosity):
    n_ax, n_az = mesh.shape["axial"], mesh.shape["azim"]
    devices = n_ax * n_az
    patches, _, section = fields.shape
    records, rows, cols = leaflet.shape
    each = max(2, 3 * patches // (2 * devices))
    slots = devices * each
    wide = -(-slots // LANES) * LANES
    height = FIELDS * section // LANES
    view = fields.reshape(patches, FIELDS, section // LANES, LANES).transpose(0, 2, 1, 3)
    view = view.reshape(patches, height, LANES)
    vmem = pl.BlockSpec(memory_space=pltpu.VMEM)
    smem = pl.BlockSpec(memory_space=pltpu.SMEM)
    out = pl.pallas_call(
        functools.partial(send_kernel, n_ax, n_az, each),
        out_shape=jax.ShapeDtypeStruct((devices, each, height, LANES), F32),
        in_specs=[vmem, smem, smem, vmem, vmem, vmem, vmem],
        out_specs=pl.BlockSpec(memory_space=pl.ANY),
        scratch_shapes=[
            pltpu.VMEM((2, records, cols), F32),
            pltpu.VMEM((records, LANES), F32),
            pltpu.VMEM((2, records, cols), BF16),
            pltpu.VMEM((records, LANES), BF16),
            pltpu.VMEM((2, records, cols), BF16),
            pltpu.VMEM((2, records, LANES), BF16),
            pltpu.VMEM((rows // 8, 8 * records, cols), F32),
            pltpu.VMEM((patches + 1, height, LANES), BF16),
            pltpu.VMEM((devices, each, height, LANES), BF16),
            pltpu.VMEM((devices, each, height, LANES), BF16),
            pltpu.VMEM((devices, each, height, LANES), F32),
            pltpu.VMEM((coarse.shape[0], 2 * FIELDS, LANES), F32),
            pltpu.VMEM((1, wide), jnp.int32),
            pltpu.SMEM((1, wide), jnp.int32),
            pltpu.SemaphoreType.DMA((4,)),
            pltpu.SemaphoreType.DMA((4,)),
            pltpu.SemaphoreType.DMA((devices - 1,)),
            pltpu.SemaphoreType.DMA((devices - 1,)),
            pltpu.SemaphoreType.DMA((devices,)),
            pltpu.SemaphoreType.DMA,
        ],
        compiler_params=pltpu.CompilerParams(
            collective_id=0, has_side_effects=True, vmem_limit_bytes=28 << 20
        ),
        name="regrid",
    )(new_owner.reshape(1, patches), coarse_of_slot, viscosity, view, leaflet, stiffness, coarse)
    out = out.reshape(slots, section // LANES, FIELDS, LANES).transpose(0, 2, 1, 3)
    return out.reshape(slots, FIELDS, section)


def solution(mesh):
    placed = (
        P(("axial", "azim"), None, None),
        P(("axial", "azim"), None),
        P(None, "axial", "azim"),
        P(),
        P(("axial", "azim"), None),
        P(("axial", "azim")),
        P(),
    )
    return jax.shard_map(
        functools.partial(shards, mesh),
        mesh=mesh,
        in_specs=placed,
        out_specs=P(("axial", "azim"), None, None),
        check_vma=False,
    )
```

time: 74.2 us -> 64 us (0.86)
  Pallas kernels: 68.2 us -> 55.6 us
  local copies, waits for them, and re-layouts: 2.55 us -> 8.03 us
  other arithmetic: 3.01 us -> 0 us
    pallas_call x1 -> x0, Pallas kernels: 16.7 us -> none  [shards(): pl.pallas_call(functools.partial(relax_kernel, group), grid=(slots // gro...]
    unnamed x0 -> x15, local copies, waits for them, and re-layouts: none -> 8.03 us
    pallas_call x1, Pallas kernels: 51.5 us -> 55.6 us  [shards(): pl.pallas_call(functools.partial(send_kernel, n_ax, n_az, each), out_shap...]
    add x2 -> x0, other arithmetic: 1.33 us -> none  [the longest x1 0.76 us: shards(): coarse_of_slot[:, None]]
    add x1 -> x0, local copies, waits for them, and re-layouts: 1.14 us -> none  [shards(): coarse_of_slot[:, None]]
    reduce_sum x2 -> x0, other arithmetic: 1.01 us -> none  [the longest x1 0.9 us: shards(): target = owners * each + jnp.sum(earlier.astype(jnp.int32), axis=1)]
    broadcast_in_dim x2 -> x0, local copies, waits for them, and re-layouts: 0.75 us -> none  [shards(): jnp.broadcast_to(jnp.tile(viscosity, height // FIELDS)[:, None], (height,...]
where the time goes in v2:
time: 64 us; the launch traced here: 63.7 us
  Pallas kernels  55.6 us (87%)
  local copies, waits for them, and re-layouts  8.03 us (13%)
    pallas_call x1, Pallas kernels, shards(): pl.pallas_call(functools.partial(send_kernel, n_ax, n_az, each), out_shap...  55.6 us
    unnamed x15, local copies, waits for them, and re-layouts  8.03 us

profile of v2, /device:TPU:17, one launch (start us, length us, event | category | flops | bytes accessed | tf_op | source)
XLA Modules:
  0.0 63.7 jit_solution(13988551617974402492)
XLA Ops:
  0.0 0.0 copy-start
  0.0 1.6 %copy-done = f32[128,4,1024]{2,1,0:T(4,128)S(1)} copy-done((f32[128,4,1024]{2,1,0:T(4,128)S(1)}, f32[128,4,1024]{2,1,0:T(4,128)}, u32[]{:S(2)}) %copy-start) | copy-done | bytes 2097176
  1.6 0.0 copy-start.1
  1.6 1.2 %copy-done.1 = bf16[64,32,256]{2,1,0:T(8,128)(2,1)S(1)} copy-done((bf16[64,32,256]{2,1,0:T(8,128)(2,1)S(1)}, bf16[64,32,256]{2,1,0:T(8,128)(2,1)}, u32[]{:S(2)}) %copy-start.1) | copy-done | bytes 1048600
  2.8 0.0 copy-start.2
  2.8 0.8 %copy-done.2 = f32[64,256]{1,0:T(8,128)S(1)} copy-done((f32[64,256]{1,0:T(8,128)S(1)}, f32[64,256]{1,0:T(8,128)}, u32[]{:S(2)}) %copy-start.2) | copy-done | bytes 65560
  3.7 0.0 copy-start.3
  3.7 0.7 %copy-done.3 = bf16[64,64]{1,0:T(8,128)(2,1)S(1)} copy-done((bf16[64,64]{1,0:T(8,128)(2,1)S(1)}, bf16[64,64]{1,0:T(8,128)(2,1)}, u32[]{:S(2)}) %copy-start.3) | copy-done | bytes 8216
  4.4 0.0 copy-start.4
  4.4 0.7 %copy-done.4 = s32[192]{0:T(256)S(1)} copy-done((s32[192]{0:T(256)S(1)}, s32[192]{0:T(256)}, u32[]{:S(2)}) %copy-start.4) | copy-done | bytes 792
  5.1 0.0 copy-start.5
  5.1 0.7 %copy-done.5 = s32[128,1]{0,1:T(1,128)S(1)} copy-done((s32[128,1]{0,1:T(1,128)S(1)}, s32[128,1]{0,1:T(1,128)}, u32[]{:S(2)}) %copy-start.5) | copy-done | bytes 536
  5.7 0.0 copy-start.6
  5.7 0.7 %copy-done.6 = f32[4]{0:T(128)S(1)} copy-done((f32[4]{0:T(128)S(1)}, f32[4]{0:T(128)}, u32[]{:S(2)}) %copy-start.6) | copy-done | bytes 40
  6.4 55.6 %regrid.1 = f32[32,6,32,128]{3,2,1,0:T(8,128)S(1)} custom-call(s32[1,128]{1,0:T(1,128)S(1)} %bitcast.13, s32[192]{0:T(256)S(1)} %copy-done.4, f32[4]{0:T(128)S(1)} %copy-done.6, f32[128,32,128]{2,1,0:T(8,128)S(1)} %bitcast.12, bf16[64,32,256]{2,1,0:T(8,128)(2,1)S(1)} %copy-done.1, bf16[64,64]{1,0:T(8,128)(2,1)S(1)} %copy-done.3, f32[64,256]{1,0:T(8,128)S(1)} %copy-done.2), custom_call_target="tpu_custom_call" | custom-call | tf_op jit(solution)/shard_map/regrid/pallas_call | solution.py:317
  62.0 1.7 %copy.11 = f32[192,4,1024]{2,1,0:T(4,128)} copy(f32[192,4,1024]{2,1,0:T(4,128)S(1)} %bitcast.11) | data formatting | bytes 6291456
Async XLA Ops:
  0.0 1.6 %copy-start = (f32[128,4,1024]{2,1,0:T(4,128)S(1)}, f32[128,4,1024]{2,1,0:T(4,128)}, u32[]{:S(2)}) copy-start(f32[128,4,1024]{2,1,0:T(4,128)} %param.7) | copy-start | bytes 6291460
  1.6 1.2 %copy-start.1 = (bf16[64,32,256]{2,1,0:T(8,128)(2,1)S(1)}, bf16[64,32,256]{2,1,0:T(8,128)(2,1)}, u32[]{:S(2)}) copy-start(bf16[64,32,256]{2,1,0:T(8,128)(2,1)} %leaf_ref.1) | copy-start | bytes 3145732
  2.8 0.8 %copy-start.2 = (f32[64,256]{1,0:T(8,128)S(1)}, f32[64,256]{1,0:T(8,128)}, u32[]{:S(2)}) copy-start(f32[64,256]{1,0:T(8,128)} %coarse_ref.1) | copy-start | bytes 196612
  3.7 0.7 %copy-start.3 = (bf16[64,64]{1,0:T(8,128)(2,1)S(1)}, bf16[64,64]{1,0:T(8,128)(2,1)}, u32[]{:S(2)}) copy-start(bf16[64,64]{1,0:T(8,128)(2,1)} %stiff_ref.1) | copy-start | bytes 24580
  4.4 0.7 %copy-start.4 = (s32[192]{0:T(256)S(1)}, s32[192]{0:T(256)}, u32[]{:S(2)}) copy-start(s32[192]{0:T(256)} %slot_ref.1) | copy-start | bytes 2308
  5.1 0.7 %copy-start.5 = (s32[128,1]{0,1:T(1,128)S(1)}, s32[128,1]{0,1:T(1,128)}, u32[]{:S(2)}) copy-start(s32[128,1]{0,1:T(1,128)} %param.8) | copy-start | bytes 1540
  5.7 0.7 %copy-start.6 = (f32[4]{0:T(128)S(1)}, f32[4]{0:T(128)}, u32[]{:S(2)}) copy-start(f32[4]{0:T(128)} %nu_ref.1) | copy-start | bytes 52

commit v3 on v2

--- a/solution.py
+++ b/solution.py
@@ -27,10 +27,11 @@
 
 
 def send_kernel(
-    n_ax, n_az, each, owner_ref, slot_ref, nu_ref, fields_ref, leaf_ref, stiff_ref, coarse_ref, out_ref,
+    n_ax, n_az, each, owner_hbm, slot_hbm, nu_hbm, fields_hbm, leaf_hbm, stiff_hbm, coarse_hbm, out_ref,
+    owner_ref, slot_ref, nu_ref, fields_ref, leaf_ref, stiff_ref, coarse_ref, load_sem,
     rows_f, cols_f, edge_rows, edge_cols, got_rows, got_cols, lap_ref, forced_ref, packed_ref,
     landed_ref, done_ref, strip_ref, pick_row, pick_ref,
-    halo_send, halo_recv, send_sem, recv_sem, out_sem, pick_sem,
+    halo_send, halo_recv, send_sem, recv_sem, out_sem, pick_sem, closed_sem,
 ):
     a = lax.axis_index("axial")
     z = lax.axis_index("azim")
@@ -40,18 +41,22 @@
     patches, height, _ = fields_ref.shape
     blocks = rows // 8
 
+    pairs_in = (
+        (leaf_hbm, leaf_ref), (stiff_hbm, stiff_ref), (owner_hbm, owner_ref), (coarse_hbm, coarse_ref),
+        (slot_hbm, slot_ref), (nu_hbm, nu_ref), (fields_hbm, fields_ref),
+    )
+    loads = [
+        pltpu.make_async_copy(src, dst, load_sem.at[i]) for i, (src, dst) in enumerate(pairs_in)
+    ]
+    for load in loads:
+        load.start()
     got_rows[...] = jnp.zeros_like(got_rows)
     barrier = pltpu.get_barrier_semaphore()
 
-    def greet(i, carry):
-        da, dz = peer(i, n_ax, n_az)
-        pl.semaphore_signal(
-            barrier, inc=1,
-            device_id=(lax.rem(a + da, n_ax), lax.rem(z + dz, n_az)), device_id_type=MESH,
-        )
-        return carry
-
-    lax.fori_loop(0, devices - 1, greet, 0)
+    row_peers = [(a, lax.rem(z + dz, n_az)) for dz in range(1, n_az)]
+    column_peers = [(lax.rem(a + da, n_ax), z) for da in range(1, n_ax)]
+    for other in row_peers + column_peers:
+        pl.semaphore_signal(barrier, inc=1, device_id=other, device_id_type=MESH)
 
     row_id = iota((rows, LANES), 0)
     lane_id = iota((rows, LANES), 1)
@@ -68,10 +73,28 @@
         cols_f[pl.ds(k, 1), :] = jnp.sum(both, axis=0, keepdims=True)
         return carry
 
+    loads[0].wait()
     lax.fori_loop(0, records, edges, 0, unroll=4)
     edge_rows[...] = rows_f[...].astype(BF16)
     edge_cols[...] = cols_f[...].astype(BF16)
-    pl.semaphore_wait(barrier, devices - 1)
+    wide_row = iota((rows, cols), 0)
+    wide_lane = iota((rows, cols), 1)
+
+    def laplace(k, carry):
+        x = leaf_ref[k].astype(F32)
+        north = jnp.where(wide_row == 0, 0.0, pltpu.roll(x, 1, 0))
+        south = jnp.where(wide_row == rows - 1, 0.0, pltpu.roll(x, rows - 1, 0))
+        west = jnp.where(wide_lane == 0, 0.0, pltpu.roll(x, 1, 1))
+        east = jnp.where(wide_lane == cols - 1, 0.0, pltpu.roll(x, cols - 1, 1))
+        total = south + north + west + east - 4.0 * x
+        for b in range(blocks):
+            lap_ref[b, pl.ds(pl.multiple_of(k * 8, 8), 8), :] = total[b * 8:(b + 1) * 8, :]
+        return carry
+
+    lax.fori_loop(0, records // 2, laplace, 0, unroll=4)
+    pl.semaphore_wait(barrier, len(row_peers) + len(column_peers))
+    for other in row_peers:
+        pl.semaphore_signal(closed_sem, inc=1, device_id=other, device_id_type=MESH)
 
     def halo(src, dst, i, device):
         return pltpu.make_async_remote_copy(
@@ -95,6 +118,9 @@
     right.start()
     left.start()
 
+    lax.fori_loop(records // 2, records, laplace, 0, unroll=4)
+    for load in loads[1:6]:
+        load.wait()
     pairs = records // FIELDS // 2
     width = pairs * FIELDS
     big = 8 * records
@@ -140,25 +166,27 @@
     left.wait_send()
     rows_f[...] = rows_f2
     cols_f[...] = jnp.where(iota(cols_l.shape, 1) < rows, cols_r, cols_l)
-    wide_row = iota((rows, cols), 0)
-    wide_lane = iota((rows, cols), 1)
-
-    def laplace(k, carry):
-        x = leaf_ref[k].astype(F32)
+    first_row = iota((8, cols), 0) == 0
+    last_row = iota((8, cols), 0) == 7
+    first_lane = lane_id == 0
+    last_lane = lane_id == LANES - 1
+
+    def sides(k, carry):
         halo_cols = jnp.broadcast_to(cols_f[pl.ds(k, 1), :], (rows, LANES))
         after = jnp.sum(jnp.where(eye_low, halo_cols, 0.0), axis=1, keepdims=True)
         before = jnp.sum(jnp.where(eye_high, halo_cols, 0.0), axis=1, keepdims=True)
-        north = jnp.where(wide_row == 0, rows_f[0, pl.ds(k, 1), :], pltpu.roll(x, 1, 0))
-        south = jnp.where(wide_row == rows - 1, rows_f[1, pl.ds(k, 1), :], pltpu.roll(x, rows - 1, 0))
-        west = jnp.where(wide_lane == 0, before, pltpu.roll(x, 1, 1))
-        east = jnp.where(wide_lane == cols - 1, after, pltpu.roll(x, cols - 1, 1))
-        total = south + north + west + east - 4.0 * x
+        west = jnp.where(first_lane, before, 0.0)
+        east = jnp.where(last_lane, after, 0.0)
+        here = pl.ds(pl.multiple_of(k * 8, 8), 8)
+        lap_ref[0, here, :] += jnp.where(first_row, rows_f[0, pl.ds(k, 1), :], 0.0)
+        lap_ref[blocks - 1, here, :] += jnp.where(last_row, rows_f[1, pl.ds(k, 1), :], 0.0)
         for b in range(blocks):
-            lap_ref[b, pl.ds(pl.multiple_of(k * 8, 8), 8), :] = total[b * 8:(b + 1) * 8, :]
-        return carry
-
-    lax.fori_loop(0, records, laplace, 0, unroll=4)
-
+            lap_ref[b, here, :LANES] += west[b * 8:(b + 1) * 8]
+            lap_ref[b, here, cols - LANES:] += east[b * 8:(b + 1) * 8]
+        return carry
+
+    lax.fori_loop(0, records, sides, 0, unroll=8)
+    loads[6].wait()
     low = iota((width, LANES), 1) < PC
     across = cols // PC
 
@@ -179,6 +207,7 @@
     lax.fori_loop(0, blocks, force, 0)
 
     picked.wait()
+    pl.semaphore_wait(closed_sem, len(row_peers))
 
     def outgoing(i):
         da, dz = peer(i, n_ax, n_az)
@@ -312,14 +341,20 @@
     height = FIELDS * section // LANES
     view = fields.reshape(patches, FIELDS, section // LANES, LANES).transpose(0, 2, 1, 3)
     view = view.reshape(patches, height, LANES)
-    vmem = pl.BlockSpec(memory_space=pltpu.VMEM)
-    smem = pl.BlockSpec(memory_space=pltpu.SMEM)
     out = pl.pallas_call(
         functools.partial(send_kernel, n_ax, n_az, each),
         out_shape=jax.ShapeDtypeStruct((devices, each, height, LANES), F32),
-        in_specs=[vmem, smem, smem, vmem, vmem, vmem, vmem],
+        in_specs=[pl.BlockSpec(memory_space=pltpu.HBM)] * 7,
         out_specs=pl.BlockSpec(memory_space=pl.ANY),
         scratch_shapes=[
+            pltpu.VMEM((1, patches), jnp.int32),
+            pltpu.SMEM((slots,), jnp.int32),
+            pltpu.SMEM((FIELDS,), F32),
+            pltpu.VMEM((patches, height, LANES), F32),
+            pltpu.VMEM(leaflet.shape, BF16),
+            pltpu.VMEM(stiffness.shape, BF16),
+            pltpu.VMEM(coarse.shape, F32),
+            pltpu.SemaphoreType.DMA((7,)),
             pltpu.VMEM((2, records, cols), F32),
             pltpu.VMEM((records, LANES), F32),
             pltpu.VMEM((2, records, cols), BF16),
@@ -340,9 +375,10 @@
             pltpu.SemaphoreType.DMA((devices - 1,)),
             pltpu.SemaphoreType.DMA((devices,)),
             pltpu.SemaphoreType.DMA,
+            pltpu.SemaphoreType.REGULAR,
         ],
         compiler_params=pltpu.CompilerParams(
-            collective_id=0, has_side_effects=True, vmem_limit_bytes=28 << 20
+            collective_id=0, has_side_effects=True, vmem_limit_bytes=62 << 20
         ),
         name="regrid",
     )(new_owner.reshape(1, patches), coarse_of_slot, viscosity, view, leaflet, stiffness, coarse)

time: 64 us -> 55.4 us (0.87)
  Pallas kernels: 55.6 us -> 51 us
  local copies, waits for them, and re-layouts: 8.03 us -> 4.24 us
    pallas_call x1, Pallas kernels: 55.6 us -> 51 us  [shards(): pl.pallas_call(functools.partial(send_kernel, n_ax, n_az, each), out_shap...]
    unnamed x15 -> x1, local copies, waits for them, and re-layouts: 8.03 us -> 4.24 us
where the time goes in v3:
time: 55.4 us; the launch traced here: 55.3 us
  Pallas kernels  51 us (92%)
  local copies, waits for them, and re-layouts  4.24 us (8%)
    pallas_call x1, Pallas kernels, shards(): pl.pallas_call(functools.partial(send_kernel, n_ax, n_az, each), out_shap...  51 us
    unnamed x1, local copies, waits for them, and re-layouts  4.24 us

profile of v3, /device:TPU:17, one launch (start us, length us, event | category | flops | bytes accessed | tf_op | source)
XLA Modules:
  0.0 55.3 jit_solution(1352207825939548552)
XLA Ops:
  0.0 51.0 %regrid.1 = f32[32,6,32,128]{3,2,1,0:T(8,128)} custom-call(s32[1,128]{1,0:T(1,128)} %bitcast.13, s32[192]{0:T(256)} %slot_hbm.1, f32[4]{0:T(128)} %nu_hbm.1, f32[128,32,128]{2,1,0:T(8,128)} %bitcast.12, bf16[64,32,256]{2,1,0:T(8,128)(2,1)} %leaf_hbm.1, bf16[64,64]{1,0:T(8,128)(2,1)} %stiff_hbm.1, f32[64,256]{1,0:T(8,128)} %coarse_hbm.1), custom_call_target="tpu_custom_call" | custom-call | tf_op jit(solution)/shard_map/regrid/pallas_call | solution.py:344
  51.0 4.2 %copy.11 = f32[192,4,1024]{2,1,0:T(4,128)} copy(f32[192,4,1024]{2,1,0:T(4,128)} %bitcast.11) | data formatting | bytes 6291456

commit v4 on v3

--- a/solution.py
+++ b/solution.py
@@ -242,7 +242,8 @@
         done_ref[me, k] = relax(block, ghost, nu)
     written(me).start()
 
-    def arrive(i, carry):
+    def arrive(turn, carry):
+        i = lax.rem(turn + devices - n_az, devices - 1)
         da, dz = peer(i, n_ax, n_az)
         source = lax.rem(a + n_ax - da, n_ax) * n_az + lax.rem(z + n_az - dz, n_az)
         pltpu.make_async_remote_copy(

time: 55.4 us -> 53.7 us (0.969)
  Pallas kernels: 51 us -> 49.3 us
    pallas_call x1, Pallas kernels: 51 us -> 49.3 us  [shards(): pl.pallas_call(functools.partial(send_kernel, n_ax, n_az, each), out_shap...]
where the time goes in v4:
time: 53.7 us; the launch traced here: 53.5 us
  Pallas kernels  49.3 us (92%)
  local copies, waits for them, and re-layouts  4.24 us (8%)
    pallas_call x1, Pallas kernels, shards(): pl.pallas_call(functools.partial(send_kernel, n_ax, n_az, each), out_shap...  49.3 us
    unnamed x1, local copies, waits for them, and re-layouts  4.24 us

profile of v4, /device:TPU:17, one launch (start us, length us, event | category | flops | bytes accessed | tf_op | source)
XLA Modules:
  0.0 53.5 jit_solution(15849491525188280450)
XLA Ops:
  0.0 49.3 %regrid.1 = f32[32,6,32,128]{3,2,1,0:T(8,128)} custom-call(s32[1,128]{1,0:T(1,128)} %bitcast.13, s32[192]{0:T(256)} %slot_hbm.1, f32[4]{0:T(128)} %nu_hbm.1, f32[128,32,128]{2,1,0:T(8,128)} %bitcast.12, bf16[64,32,256]{2,1,0:T(8,128)(2,1)} %leaf_hbm.1, bf16[64,64]{1,0:T(8,128)(2,1)} %stiff_hbm.1, f32[64,256]{1,0:T(8,128)} %coarse_hbm.1), custom_call_target="tpu_custom_call" | custom-call | tf_op jit(solution)/shard_map/regrid/pallas_call | solution.py:345
  49.3 4.2 %copy.11 = f32[192,4,1024]{2,1,0:T(4,128)} copy(f32[192,4,1024]{2,1,0:T(4,128)} %bitcast.11) | data formatting | bytes 6291456
